TPU v7x, 32 devices: a whole 2x2x4 slice. The times are simulated.
32 devices in a mesh: group: 2 (over x), gx: 16 (over z, y, core).
Axes of the slice: x: 2, y: 2, z: 4, core: 2. Of those that a mesh axis runs over, the one named last changes fastest.
Arguments:
- features: bfloat16 [192, 256, 16, 128], P(('group', 'gx')), parts along dimension 0, may hold values from -6 to 6
- occupancy: int32 [192, 256, 16], P(('group', 'gx')), parts along dimension 0, may hold values from 0 to 3
- heights: int32 [192, 256], P(('group', 'gx')), parts along dimension 0, may hold values from 0 to 16, as said below
- xy_in: bfloat16 [128, 512], replicated, may hold values from -0.5 to 0.5
- xy_out: bfloat16 [512, 128], replicated, may hold values from -0.25 to 0.25
- xz_in: bfloat16 [128, 512], replicated, may hold values from -0.5 to 0.5
- xz_out: bfloat16 [512, 128], replicated, may hold values from -0.25 to 0.25
- yz_in: bfloat16 [128, 512], replicated, may hold values from -0.5 to 0.5
- yz_out: bfloat16 [512, 128], replicated, may hold values from -0.25 to 0.25
- voxel_in: bfloat16 [128, 256], replicated, may hold values from -0.5 to 0.5
- voxel_out: bfloat16 [256, 128], replicated, may hold values from -0.375 to 0.375
Outputs:
- encoded: bfloat16 [192, 256, 16, 128], P(('group', 'gx')), parts along dimension 0
There are 2 independent parts, one for each index of `group`. A program takes and returns all parts, laid end to end along the dimension named above; an argument that names none is the same for every part. Nothing has to cross between parts.
Inputs may be any that keep to these rules, and one draw needn't show every extreme that they name: `heights`: cells of a column with height index below its valid height count.
All inputs are finite; a program needn't handle non-finite values.
Results may differ from a plain program's by a relative error of at most 0.0073.
Values may be sent and summed in bfloat16 or wider, within the bound.
No kernel may reach another device: no remote copies, remote signals or barrier semaphores. Data moves between devices by JAX's collectives and lax.ppermute only.
A program may use at most 64 MiB of HBM per device.

v0:
```python
import functools

import jax
import jax.numpy as jnp
from jax import lax
from jax.experimental import pallas as pl
from jax.experimental.pallas import tpu as pltpu
from jax.sharding import PartitionSpec as P


BF = jnp.bfloat16
F32 = jnp.float32


def radices(n):
    digits, left = [2], n // 2
    while left > 1:
        digits.append(4 if left % 4 == 0 else 2)
        left //= digits[-1]
    return digits


def mask(digit, weight):
    return digit * weight ^ (1 if weight == 2 else 0)


def offset(pos, n):
    off, slower, weight = 0, n, 1
    for digit in radices(n):
        slower //= digit
        value = (pos // slower) % digit
        crossed = jnp.minimum(value, 1) if weight == 2 else 0
        off = off ^ (value * weight) ^ crossed
        weight *= digit
    return off


def silu(half):
    return half + half * jnp.tanh(half)


def mlp(x, w_in, w_out):
    hidden = silu(jnp.dot(x, w_in, preferred_element_type=F32)).astype(BF)
    return jnp.dot(hidden, w_out, preferred_element_type=F32).astype(BF)


def position(off, n):
    pos, slower, weight, core = 0, n, 1, off % 2
    for digit in radices(n):
        slower //= digit
        if weight > 1:
            value = (off // weight) % digit
            pos = pos + value * slower
            core = core ^ jnp.minimum(value, 1) if weight == 2 else core
        weight *= digit
    return pos + core * (n // 2)


def sum_tiles(n, split, pos0, me, feat_ref, by_cell_ref, seen_ref, part_ref, even_ref, odd_ref, wait):
    rows, y_len, zs, chans = feat_ref.shape
    ys = y_len // n
    tiles, cells, stack = by_cell_ref.shape
    tile_y, lanes = cells // zs, chans
    group = min(ys, tile_y)
    share = radices(n)[-1]
    block = share * ys * zs
    steps = part_ref.shape[0] * share if split else tiles
    iota = lambda axis: lax.broadcasted_iota(jnp.int32, (stack, rows * chans), axis)
    widen = (iota(0) // zs == iota(1) // chans).astype(F32).astype(BF)

    def tile_of(i):
        return offset(pos0 + i, n) ^ me if split else i

    def expand(i, wide_ref):
        wide_ref[...] = jnp.dot(by_cell_ref[tile_of(i)], widen, preferred_element_type=F32)

    def tile(i, wide_ref):
        first = tile_of(i) * tile_y
        for g in range(tile_y // group):
            start = first + g * group
            home, inner = i if split else position((start // ys) ^ me, n), start % ys
            sub = home % share
            base = sub * ys * zs + (0 if group == ys else inner * zs)
            for y in range(group):
                cell = (g * group + y) * zs
                total = None
                for x in range(rows):
                    weight = wide_ref[cell : cell + zs, x * chans : (x + 1) * chans]
                    term = feat_ref[x, start + y].astype(F32) * weight
                    total = term if total is None else total + term
                at = pl.multiple_of(base + y * zs, zs)
                part_ref[home // share, pl.ds(at, zs), :] = total.astype(BF)
            shift = lax.rem(2 * lanes + sub * ys - lax.rem(start - inner, lanes), lanes)
            counts = pltpu.roll(seen_ref[start // lanes], shift, 1)
            kept = part_ref[home // share, block:, :].astype(F32)
            counts = jnp.where(lax.broadcasted_iota(jnp.int32, counts.shape, 1) // ys == sub, counts, kept)
            part_ref[home // share, block:, :] = counts.astype(BF)

    def pair(p, _):
        i = 2 * p
        wait(tile_of(i))
        wait(tile_of(i + 1))
        expand(i + 1, odd_ref)
        tile(i, even_ref)
        expand(jnp.minimum(i + 2, steps - 1), even_ref)
        tile(i + 1, odd_ref)

    expand(0, even_ref)
    lax.fori_loop(0, steps // 2, pair, None)


def partial_body(
    n, split, me_ref, feat_hbm, occ_hbm, hgt_hbm, part_ref, by_z_ref, feat_ref, by_cell_ref, seen_ref,
    occ_ref, hgt_ref, even_ref, odd_ref, feat_sems, side_sems,
):
    rows, y_len, zs, chans = feat_ref.shape
    tiles, cells, _ = by_cell_ref.shape
    tile_y, lanes, stack = cells // zs, chans, rows * zs
    me = me_ref[0]

    def fetch(t):
        at = pl.ds(t * tile_y, tile_y)
        return pltpu.make_async_copy(feat_hbm.at[:, at], feat_ref.at[:, at], feat_sems.at[t])

    def tile_of(i):
        return offset((i + tiles // 2) % tiles, n) ^ me if split else i

    sides = [
        pltpu.make_async_copy(occ_hbm, occ_ref, side_sems.at[0]),
        pltpu.make_async_copy(hgt_hbm, hgt_ref, side_sems.at[1]),
    ]
    for side in sides:
        side.start()
    lax.fori_loop(0, tiles, lambda i, _: fetch(tile_of(i)).start(), None)

    iota = lambda shape, axis: lax.broadcasted_iota(jnp.int32, shape, axis)
    same_z = (iota((stack, cells), 0) % zs == iota((stack, cells), 1) % zs).astype(F32)
    zidx = iota((zs, lanes), 0)
    parts = lanes // tile_y
    spread = (iota((lanes, parts * cells), 0) == iota((lanes, parts * cells), 1) // zs).astype(F32).astype(BF)
    for side in sides:
        side.wait()

    for block in range(y_len // lanes):
        at = slice(block * lanes, (block + 1) * lanes)
        weights = [
            jnp.where(zidx < hgt_ref[x : x + 1, at], occ_ref[x, :, at], 0).astype(F32) for x in range(rows)
        ]
        seen_ref[block] = sum(weights[1:], weights[0])
        stacked = jnp.concatenate(weights, axis=0).astype(BF)
        for part in range(parts):
            columns = slice(part * cells, (part + 1) * cells)
            by_z_ref[block * parts + part] = (
                jnp.dot(stacked, spread[:, columns], preferred_element_type=F32) * same_z
            )
    for t in range(tiles):
        by_cell_ref[t] = by_z_ref[t].T.astype(BF)
    sum_tiles(
        n, split, n // 2, me, feat_ref, by_cell_ref, seen_ref, part_ref, even_ref, odd_ref, lambda t: fetch(t).wait()
    )
    if split:
        lax.fori_loop(tiles // 2, tiles, lambda i, _: fetch(tile_of(i)).wait(), None)


def own_body(n, me_ref, feat_ref, by_cell_ref, seen_ref, part_ref, even_ref, odd_ref):
    sum_tiles(
        n, True, 0, me_ref[0], feat_ref, by_cell_ref, seen_ref, part_ref, even_ref, odd_ref, lambda t: None
    )


def partials(feat, occ, hgt, me, n):
    rows, y_len, zs, chans = feat.shape
    ys = y_len // n
    tile_y = 256 // zs
    tiles, cells = y_len // tile_y, tile_y * zs
    split = ys == tile_y
    vmem = pl.BlockSpec(memory_space=pltpu.VMEM)
    hbm = pl.BlockSpec(memory_space=pltpu.MemorySpace.HBM)
    smem = pl.BlockSpec(memory_space=pltpu.SMEM)
    share = radices(n)[-1]
    block = jax.ShapeDtypeStruct(((n // 2 if split else n) // share, share * ys * zs + zs, chans), BF)
    wide = [pltpu.VMEM((cells, rows * chans), F32)] * 2
    cost = pl.CostEstimate(flops=4 * feat.size, bytes_accessed=feat.size, transcendentals=0)
    part, by_z, kept, by_cell, seen = pl.pallas_call(
        functools.partial(partial_body, n, split),
        in_specs=[smem, hbm, hbm, hbm],
        out_specs=[vmem] * 5,
        out_shape=[
            block,
            jax.ShapeDtypeStruct((tiles, rows * zs, cells), F32),
            jax.ShapeDtypeStruct(feat.shape, BF),
            jax.ShapeDtypeStruct((tiles, cells, rows * zs), BF),
            jax.ShapeDtypeStruct((y_len // chans, zs, chans), F32),
        ],
        scratch_shapes=[pltpu.VMEM(occ.shape, jnp.int32), pltpu.VMEM(hgt.shape, jnp.int32)]
        + wide
        + [pltpu.SemaphoreType.DMA((tiles,)), pltpu.SemaphoreType.DMA((2,))],
        compiler_params=pltpu.CompilerParams(vmem_limit_bytes=16 << 20),
        cost_estimate=cost,
        name="partials",
    )(me.reshape(1), *(pltpu.with_memory_space_constraint(a, pltpu.MemorySpace.HBM) for a in (feat, occ, hgt)))
    if not split:
        return part[part.shape[0] // 2 :], part[: part.shape[0] // 2], by_z, kept
    own = pl.pallas_call(
        functools.partial(own_body, n),
        in_specs=[smem] + [vmem] * 3,
        out_specs=vmem,
        out_shape=block,
        scratch_shapes=wide,
        compiler_params=pltpu.CompilerParams(vmem_limit_bytes=8 << 20),
        cost_estimate=cost,
        name="own_partials",
    )(me.reshape(1), kept, by_cell, seen)
    return part, own, by_z, kept


def pool_body(feat_ref, by_z_ref, xy_ref, xz_ref, xz_acc, xz_cnt):
    rows, _, zs, chans = feat_ref.shape
    _, _, ys, _ = xy_ref.shape
    tiles, _, cells = by_z_ref.shape
    tile_y = cells // zs
    both, group = tile_y + zs, min(ys, tile_y)
    iota = lambda axis: lax.broadcasted_iota(jnp.int32, (tile_y, cells), axis)
    same_y = (iota(0) == iota(1) // zs).astype(F32)
    ones = jnp.ones((cells, chans), BF)
    xz_acc[...] = jnp.zeros_like(xz_acc)
    xz_cnt[...] = jnp.zeros_like(xz_cnt)

    def tile(t, _):
        first = t * tile_y
        picks = []
        for x in range(rows):
            row_z = by_z_ref[t, x * zs : (x + 1) * zs]
            picks += [jnp.sum(row_z, axis=0, keepdims=True) * same_y, row_z]
        picks = jnp.concatenate(picks, axis=0).astype(BF)
        counts = jnp.dot(picks, ones, preferred_element_type=F32)
        for x in range(rows):
            pick = slice(x * both, (x + 1) * both)
            cells_x = feat_ref[x, pl.ds(first, tile_y)].reshape(cells, chans)
            sums = jnp.dot(picks[pick], cells_x, preferred_element_type=F32)
            pool = (sums[:tile_y] * lax.rsqrt(1.0 + counts[pick][:tile_y])).astype(BF)
            for g in range(tile_y // group):
                start = first + g * group
                at = slice(None) if group == ys else pl.ds(pl.multiple_of(start % ys, group), group)
                xy_ref[start // ys, x, at] = pool[g * group : (g + 1) * group]
            xz_acc[x] += sums[tile_y:]
            xz_cnt[x] += counts[pick][tile_y:]

    lax.fori_loop(0, tiles, tile, None)
    xz_ref[...] = (xz_acc[...] * lax.rsqrt(1.0 + xz_cnt[...])).astype(BF)


def pools(feat, by_z, n):
    rows, y_len, zs, chans = feat.shape
    vmem = pl.BlockSpec(memory_space=pltpu.VMEM)
    return pl.pallas_call(
        pool_body,
        in_specs=[vmem] * 2,
        out_specs=[vmem] * 2,
        out_shape=[
            jax.ShapeDtypeStruct((n, rows, y_len // n, chans), BF),
            jax.ShapeDtypeStruct((rows, zs, chans), BF),
        ],
        scratch_shapes=[pltpu.VMEM((rows, zs, chans), F32)] * 2,
        compiler_params=pltpu.CompilerParams(vmem_limit_bytes=8 << 20),
        cost_estimate=pl.CostEstimate(flops=2 * 32 * feat.size, bytes_accessed=1 << 20, transcendentals=0),
        name="pools",
    )(feat, by_z)


def planes_body(xy_ref, xz_ref, xy_in, xy_out, xz_in, xz_out, xy_plane, xz_plane):
    size = min(256, xy_ref.shape[0])
    for r in range(0, xy_ref.shape[0], size):
        xy_plane[r : r + size] = mlp(xy_ref[r : r + size], 0.5 * xy_in[...], xy_out[...])
    xz_plane[...] = mlp(xz_ref[...], 0.5 * xz_in[...], xz_out[...])


def planes(xy_pool, xz_pool, xy_in, xy_out, xz_in, xz_out):
    vmem = pl.BlockSpec(memory_space=pltpu.VMEM)
    flops = 4 * (xy_pool.size + xz_pool.size) * xy_in.shape[1]
    return pl.pallas_call(
        planes_body,
        in_specs=[vmem] * 6,
        out_specs=[vmem] * 2,
        out_shape=[jax.ShapeDtypeStruct(xy_pool.shape, BF), jax.ShapeDtypeStruct(xz_pool.shape, BF)],
        compiler_params=pltpu.CompilerParams(vmem_limit_bytes=8 << 20),
        cost_estimate=pl.CostEstimate(flops=flops, bytes_accessed=1 << 20, transcendentals=0),
        name="planes",
    )(xy_pool, xz_pool, xy_in, xy_out, xz_in, xz_out)


def yz_body(parts, zs, *refs):
    w_in, w_out, out = refs[parts:]
    count, cells, chans = out.shape
    pools = []
    ys = cells // zs
    for u in range(count):
        total, seen = 0.0, 0.0
        for v in range(parts):
            at = (u ^ v) * cells
            total = total + refs[v][0, at : at + cells].astype(F32)
            seen = seen + refs[v][0, count * cells :, (u ^ v) * ys : (u ^ v) * ys + ys].astype(F32)
        scale = lax.rsqrt(1.0 + seen)
        pools += [
            total[y * zs : (y + 1) * zs] * jnp.broadcast_to(scale[:, y : y + 1], (zs, chans)) for y in range(ys)
        ]
    pool = jnp.concatenate(pools, axis=0).astype(BF)
    out[...] = mlp(pool, 0.5 * w_in[...], w_out[...]).reshape(count, cells, chans)


def yz_mlp(parts, zs, w_in, w_out):
    vmem = pl.BlockSpec(memory_space=pltpu.VMEM)
    count, chans = len(parts), parts[0].shape[2]
    cells = (parts[0].shape[1] - zs) // count
    return pl.pallas_call(
        functools.partial(yz_body, len(parts), zs),
        in_specs=[vmem] * (len(parts) + 2),
        out_specs=vmem,
        out_shape=jax.ShapeDtypeStruct((count, cells, chans), BF),
        compiler_params=pltpu.CompilerParams(vmem_limit_bytes=8 << 20),
        cost_estimate=pl.CostEstimate(
            flops=4 * count * cells * w_in.size, bytes_accessed=1 << 19, transcendentals=0
        ),
        name="yz_mlp",
    )(*parts, w_in, w_out)


def first_body(feat_ref, xy_ref, xz_ref, w_in, out_ref):
    n, rows, ys, chans = xy_ref.shape
    zs = xz_ref.shape[1]
    half = 0.5 * w_in[...]

    def chunk(c, _):
        for x in range(rows):
            xy = xy_ref[c, x].astype(F32)
            part = feat_ref[x, pl.ds(c * ys, ys)].astype(F32) + xy[:, None, :] + xz_ref[x].astype(F32)[None]
            part = part.reshape(ys * zs, chans).astype(BF)
            out_ref[c, x] = jnp.dot(part, half, preferred_element_type=F32)

    lax.fori_loop(0, n, chunk, None)


def first_layer(feat, xy_plane, xz_plane, w_in):
    n, rows, ys, _ = xy_plane.shape
    vmem = pl.BlockSpec(memory_space=pltpu.VMEM)
    return pl.pallas_call(
        first_body,
        in_specs=[vmem] * 4,
        out_specs=vmem,
        out_shape=jax.ShapeDtypeStruct((n, rows, ys * xz_plane.shape[1], w_in.shape[1]), F32),
        compiler_params=pltpu.CompilerParams(vmem_limit_bytes=8 << 20),
        cost_estimate=pl.CostEstimate(flops=2 * feat.size * w_in.shape[1], bytes_accessed=1 << 20, transcendentals=0),
        name="first_layer",
    )(feat, xy_plane, xz_plane, w_in)


def voxel_body(n, groups, before, last, me_ref, first_ref, w_in, w_out, *refs):
    yz_refs, refs = refs[: len(groups)], refs[len(groups) :]
    if before:
        prev_ref, refs = refs[0], refs[2:]
    out_hbm, done_ref, own_ref, sems = refs
    _, rows, ys, zs, chans = done_ref.shape
    half = 0.5 * w_in[...]

    def send(source, index, pos, sem):
        at = pl.ds((offset(pos, n) ^ me_ref[0]) * ys, ys)
        return pltpu.make_async_copy(source.at[index], out_hbm.at[:, at], sems.at[sem])

    copies = [send(prev_ref, j, pos, j) for j, pos in enumerate(before)]
    for copy in copies:
        copy.start()
    slot = 0
    for yz_ref, (_, count) in zip(yz_refs, groups):
        both = yz_ref[...].reshape(count * ys * zs, chans)
        both = jnp.dot(both, half, preferred_element_type=F32)
        own_ref[slot : slot + count] = both.reshape(count, ys * zs, half.shape[1])
        slot += count
    slot = 0
    for yz_ref, (pos0, count) in zip(yz_refs, groups):

        def chunk(j, _, yz_ref=yz_ref, pos0=pos0, slot=slot):
            home = offset(pos0 + j, n) ^ me_ref[0]
            for x in range(0, rows, rows):
                hidden = silu(first_ref[home, x : x + rows] + own_ref[slot + j][None]).astype(BF)
                cells = jnp.dot(hidden.reshape(rows * ys * zs, -1), w_out[...], preferred_element_type=F32).astype(BF)
                done_ref[slot + j, x : x + rows] = cells.reshape(rows, ys, zs, chans)
            if last:
                send(done_ref, slot + j, pos0 + j, len(before) + slot + j).start()

        lax.fori_loop(0, count, chunk, None)
        slot += count
    if last:
        slot = 0
        for pos0, count in groups:
            copies += [send(done_ref, slot + j, pos0 + j, len(before) + slot + j) for j in range(count)]
            slot += count
    for copy in copies:
        copy.wait()


def voxels(state, n, groups, yz, last, me, shape, first, w_in, w_out):
    rows, y_len, zs, chans = shape
    ys, size = y_len // n, sum(count for _, count in groups)
    before, extra = ([], []) if state is None else (state[0], list(state[1:]))
    vmem = pl.BlockSpec(memory_space=pltpu.VMEM)
    hbm = pl.BlockSpec(memory_space=pltpu.MemorySpace.HBM)
    done = (size, rows, ys, zs, chans)
    operands = [me.reshape(1), first, w_in, w_out, *yz, *extra]
    sems = pltpu.SemaphoreType.DMA((len(before) + (size if last else 0) or 1,))
    out = pl.pallas_call(
        functools.partial(voxel_body, n, groups, before, last),
        in_specs=[pl.BlockSpec(memory_space=pltpu.SMEM)] + [vmem] * (3 + len(yz)) + [vmem, hbm][: len(extra)],
        out_specs=[hbm] if last else [hbm, vmem],
        out_shape=[jax.ShapeDtypeStruct(shape, BF)] + ([] if last else [jax.ShapeDtypeStruct(done, BF)]),
        scratch_shapes=([pltpu.VMEM(done, BF)] if last else [])
        + [pltpu.VMEM((size, ys * zs, w_in.shape[1]), F32), sems],
        input_output_aliases={len(operands) - 1: 0} if extra else {},
        compiler_params=pltpu.CompilerParams(vmem_limit_bytes=20 << 20, has_side_effects=True),
        cost_estimate=pl.CostEstimate(
            flops=4 * size * rows * ys * zs * w_in.size, bytes_accessed=1 << 20, transcendentals=0
        ),
        name="voxels",
    )(*operands)
    if last:
        return out[0]
    return [pos0 + j for pos0, count in groups for j in range(count)], out[1], out[0]


def swap(value, n, offset):
    return lax.ppermute(value, "gx", [(i, i ^ offset) for i in range(n)])


def per_device(n, features, occupancy, heights, xy_in, xy_out, xz_in, xz_out, yz_in, yz_out, voxel_in, voxel_out):
    zs = features.shape[2]
    me = lax.axis_index("gx")
    theirs, held, by_z, feat = partials(features, jnp.swapaxes(occupancy, 1, 2), heights, me, n)
    chans = features.shape[3]

    digits = radices(n)
    weights = [1]
    for digit in digits:
        weights.append(weights[-1] * digit)
    for stage, digit in enumerate(digits[:-1]):
        size = held.shape[0] // digit
        if stage == 0:
            pieces = [held, swap(theirs, n, 1)]
        else:
            pieces = [held[:size]] + [
                swap(held[d * size : (d + 1) * size], n, mask(d, weights[stage])) for d in range(1, digit)
            ]
        if stage == 1:
            pieces, xy_plane, xz_plane = lax.optimization_barrier((pieces, xy_plane, xz_plane))
        held = sum(piece.astype(F32) for piece in pieces).astype(BF)
        if stage == 0:
            held, by_z = lax.optimization_barrier((held, by_z))
            xy_pool, xz_pool = pools(feat, by_z, n)
            xy_plane, xz_plane = planes(
                xy_pool.reshape(-1, chans), xz_pool.reshape(-1, chans), xy_in, xy_out, xz_in, xz_out
            )
    first = first_layer(feat, xy_plane.reshape(xy_pool.shape), xz_plane.reshape(xz_pool.shape), voxel_in)
    slower = digits[-1]
    assert held.shape[0] == 1
    pieces = [held] + [swap(held, n, mask(d, weights[len(digits) - 1])) for d in range(1, slower)]
    pieces, first = lax.optimization_barrier((pieces, first))
    plane = yz_mlp(pieces, zs, yz_in, yz_out)

    call = functools.partial(voxels, me=me, shape=features.shape, first=first, w_in=voxel_in, w_out=voxel_out)
    sibling = n // 2
    passed = swap(plane, n, 1)
    state = call(None, n, [(0, slower)], [plane], False)
    state = call(state, n, [(sibling, slower)], [passed], False)
    waiting = []
    for stage, digit in reversed(list(enumerate(digits))[1:-1]):
        arrived = []
        for d in range(1, digit):
            arrived.append(swap(plane, n, mask(d, weights[stage])))
        for d, piece in enumerate(arrived, 1):
            piece, *tail = lax.optimization_barrier((piece, *state[1:]))
            state = (state[0], *tail)
            pieces = waiting + [((d * slower, slower), piece)]
            waiting = [((sibling + d * slower, slower), swap(piece, n, 1))]
            state = call(state, n, [g for g, _ in pieces], [p for _, p in pieces], False)
        plane = jnp.concatenate([plane] + arrived, axis=0)
        slower *= digit
    return call(state, n, [g for g, _ in waiting], [p for _, p in waiting], True)


def solution(mesh):
    split = ("group", "gx")
    in_specs = (P(split, None, None, None), P(split, None, None), P(split, None)) + (P(),) * 8
    n = mesh.shape["gx"]

    def body(*args):
        return per_device(n, *args)

    step = jax.shard_map(
        body, mesh=mesh, in_specs=in_specs, out_specs=P(split, None, None, None), check_vma=False
    )
    if len(radices(n)) > 3:
        return step
    return step
```

profile of v0, /device:TPU:0, one launch (start us, length us, event | category | flops | bytes accessed | tf_op | source)
XLA Modules:
  0.0 43.7 jit_solution(8689902719486486899)
XLA Ops:
  0.0 3.6 %partials.1 = (bf16[4,528,128]{2,1,0:T(8,128)(2,1)S(1)}, f32[16,96,256]{2,1,0:T(8,128)S(1)}, bf16[6,256,16,128]{3,2,1,0:T(8,128)(2,1)S(1)}, bf16[16,256,96]{2,1,0:T(8,128)(2,1)S(1)}, f32[2,16,128]{2,1,0:T(8,128)S(1)}) custom-call(s32[1]{0:T(128)} %bitcast.me_ref, bf16[6,256,16,128]{3,2,1,0:T(8,128)(2,1)} %feat_hbm.1, s32[6,16,256]{2,1,0:T(8,128)} %bitcast.10, ...), custom_call_target="tpu_custom_call" | custom-call | flops 12582912 | bytes 3145728 | tf_op jit(solution)/shard_map/partials/pallas_call | solution.py:184
  3.7 0.6 %collective-permute-start = (bf16[4,528,128]{2,1,0:T(8,128)(2,1)S(1)}, bf16[4,528,128]{2,1,0:T(8,128)(2,1)S(1)}, u32[]{:S(2)}, u32[]{:S(2)}) collective-permute-start(bf16[4,528,128]{2,1,0:T(8,128)(2,1)S(1)} %get-tuple-element.47), channel_id=1, source_target_pairs={{0,1},{1,0},{2,3},{3,2},{4,5},{5,4},{6,7},{7,6},{8,9},{9,8},{10,11... | collective-permute-start | bytes 1622024 | tf_op jit(solution)/shard_map/ppermute | solution.py:430
  4.2 1.7 %own_partials.1 = bf16[4,528,128]{2,1,0:T(8,128)(2,1)S(1)} custom-call(s32[1]{0:T(128)} %bitcast.me_ref, bf16[6,256,16,128]{3,2,1,0:T(8,128)(2,1)S(1)} %get-tuple-element.44.feat_ref, bf16[16,256,96]{2,1,0:T(8,128)(2,1)S(1)} %get-tuple-element.45.by_cell_ref, f32[2,16,128]{2,1,0:T(8,128)S(1)} %get-tuple-element.46.seen_ref), custom_call_target="tpu_custom_call" | custom-call | flops 12582912 | bytes 3145728 | tf_op jit(solution)/shard_map/own_partials/pallas_call | solution.py:204
  5.9 0.0 copy-start.4
  6.0 0.0 copy-start.5
  6.0 0.0 copy-start.6
  6.0 0.0 copy-start.7
  6.0 0.0 copy-start
  6.0 0.0 collective-permute-done
  6.0 0.1 add_convert_fusion
  6.2 3.7 %collective-permute-start.3 = (bf16[1,528,128]{2,1,0:T(8,128)(2,1)S(1)}, bf16[1,528,128]{2,1,0:T(8,128)(2,1)S(1)}, u32[]{:S(2)}, u32[]{:S(2)}) collective-permute-start(bf16[1,528,128]{2,1,0:T(8,128)(2,1)S(1)} %get-tuple-element.83), channel_id=1, source_target_pairs={{0,7},{1,6},{2,5},{3,4},{4,3},{5,2},{6,1},{7,0},{8,15},{9,14},{10,... | collective-permute-start | bytes 405512 | tf_op jit(solution)/shard_map/ppermute | solution.py:430
  9.9 0.2 collective-permute-start.2
  10.1 0.2 collective-permute-start.1
  10.3 3.5 %pools.1 = (bf16[16,6,16,128]{3,2,1,0:T(8,128)(2,1)S(1)}, bf16[6,16,128]{2,1,0:T(8,128)(2,1)S(1)}) custom-call(bf16[6,256,16,128]{3,2,1,0:T(8,128)(2,1)S(1)} %get-tuple-element.44.feat_ref, f32[16,96,256]{2,1,0:T(8,128)S(1)} %get-tuple-element.50.by_z_ref), custom_call_target="tpu_custom_call" | custom-call | flops 201326592 | bytes 1048576 | tf_op jit(solution)/shard_map/pools/pallas_call | solution.py:256
  13.8 0.0 copy-done.4
  13.8 0.0 copy-done.5
  13.8 0.0 copy-done.6
  13.8 0.0 copy-done.7
  13.8 1.7 %planes.1 = (bf16[1536,128]{1,0:T(8,128)(2,1)S(1)}, bf16[96,128]{1,0:T(8,128)(2,1)S(1)}) custom-call(bf16[1536,128]{1,0:T(8,128)(2,1)S(1)} %bitcast.8, bf16[96,128]{1,0:T(8,128)(2,1)S(1)} %bitcast.9, bf16[128,512]{1,0:T(8,128)(2,1)S(1)} %copy-done.4, bf16[512,128]{1,0:T(8,128)(2,1)S(1)} %copy-done.5, bf16[128,512]{1,0:T(8,128)(2,1)S(1)} %copy-done.6, ...), custom_call_target="tpu_custom_call" | custom-call | flops 427819008 | bytes 1048576 | tf_op jit(solution)/shard_map/planes/pallas_call | solution.py:281
  15.5 0.0 collective-permute-done.3
  15.5 1.0 %collective-permute-done.2 = bf16[1,528,128]{2,1,0:T(8,128)(2,1)S(1)} collective-permute-done((bf16[1,528,128]{2,1,0:T(8,128)(2,1)S(1)}, bf16[1,528,128]{2,1,0:T(8,128)(2,1)S(1)}, u32[]{:S(2)}, u32[]{:S(2)}) %collective-permute-start.2) | collective-permute-done | bytes 135200 | tf_op jit(solution)/shard_map/ppermute | solution.py:430
  16.6 0.3 collective-permute-done.1
  16.9 0.1 add_convert_fusion.1.refs_0_
  17.0 2.8 %collective-permute-start.4 = (bf16[1,528,128]{2,1,0:T(8,128)(2,1)S(1)}, bf16[1,528,128]{2,1,0:T(8,128)(2,1)S(1)}, u32[]{:S(2)}, u32[]{:S(2)}) collective-permute-start(bf16[1,528,128]{2,1,0:T(8,128)(2,1)S(1)} %add_convert_fusion.1.refs_0_), channel_id=1, source_target_pairs={{0,8},{1,9},{2,10},{3,11},{4,12},{5,13},{6,14},{7,15},{8,0},{9,1},... | collective-permute-start | bytes 405512 | tf_op jit(solution)/shard_map/ppermute | solution.py:430
  19.8 5.8 %first_layer.1.first_ref = f32[16,6,256,256]{3,2,1,0:T(8,128)S(1)} custom-call(bf16[6,256,16,128]{3,2,1,0:T(8,128)(2,1)S(1)} %get-tuple-element.44.feat_ref, bf16[16,6,16,128]{3,2,1,0:T(8,128)(2,1)S(1)} %bitcast.6, bf16[6,16,128]{2,1,0:T(8,128)(2,1)S(1)} %bitcast.7, bf16[128,256]{1,0:T(8,128)(2,1)S(1)} %copy-done), custom_call_target="tpu_custom_call" | custom-call | flops 1610612736 | bytes 1048576 | tf_op jit(solution)/shard_map/first_layer/pallas_call | solution.py:346
  25.6 1.0 %collective-permute-done.4.refs_1_ = bf16[1,528,128]{2,1,0:T(8,128)(2,1)S(1)} collective-permute-done((bf16[1,528,128]{2,1,0:T(8,128)(2,1)S(1)}, bf16[1,528,128]{2,1,0:T(8,128)(2,1)S(1)}, u32[]{:S(2)}, u32[]{:S(2)}) %collective-permute-start.4) | collective-permute-done | bytes 135200 | tf_op jit(solution)/shard_map/ppermute | solution.py:430
  26.5 0.0 copy-done.2
  26.5 0.6 %yz_mlp.1.refs_0_ = bf16[2,256,128]{2,1,0:T(8,128)(2,1)S(1)} custom-call(bf16[1,528,128]{2,1,0:T(8,128)(2,1)S(1)} %add_convert_fusion.1.refs_0_, bf16[1,528,128]{2,1,0:T(8,128)(2,1)S(1)} %collective-permute-done.4.refs_1_, bf16[128,512]{1,0:T(8,128)(2,1)S(1)} %copy-done.2, bf16[512,128]{1,0:T(8,128)(2,1)S(1)} %copy-done.3), custom_call_target="tpu_custom_call" | custom-call | flops 134217728 | bytes 524288 | tf_op jit(solution)/shard_map/yz_mlp/pallas_call | solution.py:315
  27.1 0.1 collective-permute-start.7
  27.2 1.7 %collective-permute-start.6 = (bf16[2,256,128]{2,1,0:T(8,128)(2,1)S(1)}, bf16[2,256,128]{2,1,0:T(8,128)(2,1)S(1)}, u32[]{:S(2)}, u32[]{:S(2)}) collective-permute-start(bf16[2,256,128]{2,1,0:T(8,128)(2,1)S(1)} %yz_mlp.1.refs_0_), channel_id=1, source_target_pairs={{0,3},{1,2},{2,1},{3,0},{4,7},{5,6},{6,5},{7,4},{8,11},{9,10},{10,... | collective-permute-start | bytes 393224 | tf_op jit(solution)/shard_map/ppermute | solution.py:430
  28.9 0.3 collective-permute-start.9
  29.2 1.1 %voxels.6 = (bf16[6,256,16,128]{3,2,1,0:T(8,128)(2,1)}, bf16[2,6,16,16,128]{4,3,2,1,0:T(8,128)(2,1)S(1)}) custom-call(s32[1]{0:T(128)} %bitcast.me_ref, f32[16,6,256,256]{3,2,1,0:T(8,128)S(1)} %first_layer.1.first_ref, bf16[128,256]{1,0:T(8,128)(2,1)S(1)} %copy-done, bf16[256,128]{1,0:T(8,128)(2,1)S(1)} %copy-done.1, bf16[2,256,128]{2,1,0:T(8,128)(2,1)S(1)} %yz_mlp.1.refs_0_), custom_call_target="tpu_custom_call" | custom-call | flops 402653184 | bytes 1048576 | tf_op jit(solution)/shard_map/voxels/pallas_call | solution.py:410
  30.3 0.0 collective-permute-done.7.refs_0_
  30.3 1.1 %voxels.7 = (bf16[6,256,16,128]{3,2,1,0:T(8,128)(2,1)}, bf16[2,6,16,16,128]{4,3,2,1,0:T(8,128)(2,1)S(1)}) custom-call(s32[1]{0:T(128)} %bitcast.me_ref, f32[16,6,256,256]{3,2,1,0:T(8,128)S(1)} %first_layer.1.first_ref, bf16[128,256]{1,0:T(8,128)(2,1)S(1)} %copy-done, bf16[256,128]{1,0:T(8,128)(2,1)S(1)} %copy-done.1, ...), custom_call_target="tpu_custom_call", output_to_operand_aliasing={{0}: (6, {})} | custom-call | flops 402653184 | bytes 1048576 | tf_op jit(solution)/shard_map/voxels/pallas_call | solution.py:410
  31.4 1.1 %collective-permute-done.6.refs_0_ = bf16[2,256,128]{2,1,0:T(8,128)(2,1)S(1)} collective-permute-done((bf16[2,256,128]{2,1,0:T(8,128)(2,1)S(1)}, bf16[2,256,128]{2,1,0:T(8,128)(2,1)S(1)}, u32[]{:S(2)}, u32[]{:S(2)}) %collective-permute-start.6) | collective-permute-done | bytes 131104 | tf_op jit(solution)/shard_map/ppermute | solution.py:430
  32.5 0.7 %collective-permute-start.8 = (bf16[2,256,128]{2,1,0:T(8,128)(2,1)S(1)}, bf16[2,256,128]{2,1,0:T(8,128)(2,1)S(1)}, u32[]{:S(2)}, u32[]{:S(2)}) collective-permute-start(bf16[2,256,128]{2,1,0:T(8,128)(2,1)S(1)} %collective-permute-done.6.refs_0_), channel_id=1, source_target_pairs={{0,1},{1,0},{2,3},{3,2},{4,5},{5,4},{6,7},{7,6},{8,9},{9,8},{10,11... | collective-permute-start | bytes 393224 | tf_op jit(solution)/shard_map/ppermute | solution.py:430
  33.2 1.3 %collective-permute-start.5 = (bf16[2,256,128]{2,1,0:T(8,128)(2,1)S(1)}, bf16[2,256,128]{2,1,0:T(8,128)(2,1)S(1)}, u32[]{:S(2)}, u32[]{:S(2)}) collective-permute-start(bf16[2,256,128]{2,1,0:T(8,128)(2,1)S(1)} %yz_mlp.1.refs_0_), channel_id=1, source_target_pairs={{0,7},{1,6},{2,5},{3,4},{4,3},{5,2},{6,1},{7,0},{8,15},{9,14},{10,... | collective-permute-start | bytes 393224 | tf_op jit(solution)/shard_map/ppermute | solution.py:430
  34.5 1.1 %voxels.8 = (bf16[6,256,16,128]{3,2,1,0:T(8,128)(2,1)}, bf16[2,6,16,16,128]{4,3,2,1,0:T(8,128)(2,1)S(1)}) custom-call(s32[1]{0:T(128)} %bitcast.me_ref, f32[16,6,256,256]{3,2,1,0:T(8,128)S(1)} %first_layer.1.first_ref, bf16[128,256]{1,0:T(8,128)(2,1)S(1)} %copy-done, bf16[256,128]{1,0:T(8,128)(2,1)S(1)} %copy-done.1, ...), custom_call_target="tpu_custom_call", output_to_operand_aliasing={{0}: (6, {})} | custom-call | flops 402653184 | bytes 1048576 | tf_op jit(solution)/shard_map/voxels/pallas_call | solution.py:410
  35.5 0.0 collective-permute-done.9.refs_1_
  35.5 0.6 %collective-permute-start.11 = (bf16[2,256,128]{2,1,0:T(8,128)(2,1)S(1)}, bf16[2,256,128]{2,1,0:T(8,128)(2,1)S(1)}, u32[]{:S(2)}, u32[]{:S(2)}) collective-permute-start(bf16[2,256,128]{2,1,0:T(8,128)(2,1)S(1)} %collective-permute-done.9.refs_1_), channel_id=1, source_target_pairs={{0,1},{1,0},{2,3},{3,2},{4,5},{5,4},{6,7},{7,6},{8,9},{9,8},{10,11... | collective-permute-start | bytes 393224 | tf_op jit(solution)/shard_map/ppermute | solution.py:430
  36.1 0.0 collective-permute-done.8.refs_0_
  36.1 2.0 %voxels.9 = (bf16[6,256,16,128]{3,2,1,0:T(8,128)(2,1)}, bf16[4,6,16,16,128]{4,3,2,1,0:T(8,128)(2,1)S(1)}) custom-call(s32[1]{0:T(128)} %bitcast.me_ref, f32[16,6,256,256]{3,2,1,0:T(8,128)S(1)} %first_layer.1.first_ref, bf16[128,256]{1,0:T(8,128)(2,1)S(1)} %copy-done, bf16[256,128]{1,0:T(8,128)(2,1)S(1)} %copy-done.1, ...), custom_call_target="tpu_custom_call", output_to_operand_aliasing={{0}: (7, {})} | custom-call | flops 805306368 | bytes 1048576 | tf_op jit(solution)/shard_map/voxels/pallas_call | solution.py:410
  38.1 1.6 %collective-permute-done.5.refs_1_ = bf16[2,256,128]{2,1,0:T(8,128)(2,1)S(1)} collective-permute-done((bf16[2,256,128]{2,1,0:T(8,128)(2,1)S(1)}, bf16[2,256,128]{2,1,0:T(8,128)(2,1)S(1)}, u32[]{:S(2)}, u32[]{:S(2)}) %collective-permute-start.5) | collective-permute-done | bytes 131104 | tf_op jit(solution)/shard_map/ppermute | solution.py:430
  39.7 0.1 collective-permute-start.10
  39.8 0.0 collective-permute-done.11.refs_0_
  39.8 2.0 %voxels.10 = (bf16[6,256,16,128]{3,2,1,0:T(8,128)(2,1)}, bf16[4,6,16,16,128]{4,3,2,1,0:T(8,128)(2,1)S(1)}) custom-call(s32[1]{0:T(128)} %bitcast.me_ref, f32[16,6,256,256]{3,2,1,0:T(8,128)S(1)} %first_layer.1.first_ref, bf16[128,256]{1,0:T(8,128)(2,1)S(1)} %copy-done, bf16[256,128]{1,0:T(8,128)(2,1)S(1)} %copy-done.1, ...), custom_call_target="tpu_custom_call", output_to_operand_aliasing={{0}: (7, {})} | custom-call | flops 805306368 | bytes 1048576 | tf_op jit(solution)/shard_map/voxels/pallas_call | solution.py:410
  41.8 0.0 collective-permute-done.10.refs_0_
  41.8 1.8 %voxels.11 = bf16[6,256,16,128]{3,2,1,0:T(8,128)(2,1)} custom-call(s32[1]{0:T(128)} %bitcast.me_ref, f32[16,6,256,256]{3,2,1,0:T(8,128)S(1)} %first_layer.1.first_ref, bf16[128,256]{1,0:T(8,128)(2,1)S(1)} %copy-done, bf16[256,128]{1,0:T(8,128)(2,1)S(1)} %copy-done.1, ...), custom_call_target="tpu_custom_call", output_to_operand_aliasing={{}: (6, {})} | custom-call | flops 402653184 | bytes 1048576 | tf_op jit(solution)/shard_map/voxels/pallas_call | solution.py:410
  (7 shorter events, 0.0 us)
Async XLA Ops:
  3.7 2.4 %collective-permute-start = (bf16[4,528,128]{2,1,0:T(8,128)(2,1)S(1)}, bf16[4,528,128]{2,1,0:T(8,128)(2,1)S(1)}, u32[]{:S(2)}, u32[]{:S(2)}) collective-permute-start(bf16[4,528,128]{2,1,0:T(8,128)(2,1)S(1)} %get-tuple-element.47), channel_id=1, source_target_pairs={{0,1},{1,0},{2,3},{3,2},{4,5},{5,4},{6,7},{7,6},{8,9},{9,8},{10,11... | collective-permute-start | bytes 1622024 | tf_op jit(solution)/shard_map/ppermute | solution.py:430
  5.9 7.9 %copy-start.4 = (bf16[128,512]{1,0:T(8,128)(2,1)S(1)}, bf16[128,512]{1,0:T(8,128)(2,1)}, u32[]{:S(2)}) copy-start(bf16[128,512]{1,0:T(8,128)(2,1)} %xy_in.1) | copy-start | bytes 393220
  6.0 7.9 %copy-start.5 = (bf16[512,128]{1,0:T(8,128)(2,1)S(1)}, bf16[512,128]{1,0:T(8,128)(2,1)}, u32[]{:S(2)}) copy-start(bf16[512,128]{1,0:T(8,128)(2,1)} %xy_out.1) | copy-start | bytes 393220
  6.0 7.9 %copy-start.6 = (bf16[128,512]{1,0:T(8,128)(2,1)S(1)}, bf16[128,512]{1,0:T(8,128)(2,1)}, u32[]{:S(2)}) copy-start(bf16[128,512]{1,0:T(8,128)(2,1)} %xz_in.1) | copy-start | bytes 393220
  6.0 7.9 %copy-start.7 = (bf16[512,128]{1,0:T(8,128)(2,1)S(1)}, bf16[512,128]{1,0:T(8,128)(2,1)}, u32[]{:S(2)}) copy-start(bf16[512,128]{1,0:T(8,128)(2,1)} %xz_out.1) | copy-start | bytes 393220
  6.0 13.8 %copy-start = (bf16[128,256]{1,0:T(8,128)(2,1)S(1)}, bf16[128,256]{1,0:T(8,128)(2,1)}, u32[]{:S(2)}) copy-start(bf16[128,256]{1,0:T(8,128)(2,1)} %w_in.13) | copy-start | bytes 196612
  6.2 9.3 %collective-permute-start.3 = (bf16[1,528,128]{2,1,0:T(8,128)(2,1)S(1)}, bf16[1,528,128]{2,1,0:T(8,128)(2,1)S(1)}, u32[]{:S(2)}, u32[]{:S(2)}) collective-permute-start(bf16[1,528,128]{2,1,0:T(8,128)(2,1)S(1)} %get-tuple-element.83), channel_id=1, source_target_pairs={{0,7},{1,6},{2,5},{3,4},{4,3},{5,2},{6,1},{7,0},{8,15},{9,14},{10,... | collective-permute-start | bytes 405512 | tf_op jit(solution)/shard_map/ppermute | solution.py:430
  9.9 6.7 %collective-permute-start.2 = (bf16[1,528,128]{2,1,0:T(8,128)(2,1)S(1)}, bf16[1,528,128]{2,1,0:T(8,128)(2,1)S(1)}, u32[]{:S(2)}, u32[]{:S(2)}) collective-permute-start(bf16[1,528,128]{2,1,0:T(8,128)(2,1)S(1)} %get-tuple-element.84), channel_id=1, source_target_pairs={{0,5},{1,4},{2,7},{3,6},{4,1},{5,0},{6,3},{7,2},{8,13},{9,12},{10,... | collective-permute-start | bytes 405512 | tf_op jit(solution)/shard_map/ppermute | solution.py:430
  10.1 6.8 %collective-permute-start.1 = (bf16[1,528,128]{2,1,0:T(8,128)(2,1)S(1)}, bf16[1,528,128]{2,1,0:T(8,128)(2,1)S(1)}, u32[]{:S(2)}, u32[]{:S(2)}) collective-permute-start(bf16[1,528,128]{2,1,0:T(8,128)(2,1)S(1)} %get-tuple-element.85), channel_id=1, source_target_pairs={{0,3},{1,2},{2,1},{3,0},{4,7},{5,6},{6,5},{7,4},{8,11},{9,10},{10,... | collective-permute-start | bytes 405512 | tf_op jit(solution)/shard_map/ppermute | solution.py:430
  17.0 9.5 %collective-permute-start.4 = (bf16[1,528,128]{2,1,0:T(8,128)(2,1)S(1)}, bf16[1,528,128]{2,1,0:T(8,128)(2,1)S(1)}, u32[]{:S(2)}, u32[]{:S(2)}) collective-permute-start(bf16[1,528,128]{2,1,0:T(8,128)(2,1)S(1)} %add_convert_fusion.1.refs_0_), channel_id=1, source_target_pairs={{0,8},{1,9},{2,10},{3,11},{4,12},{5,13},{6,14},{7,15},{8,0},{9,1},... | collective-permute-start | bytes 405512 | tf_op jit(solution)/shard_map/ppermute | solution.py:430
  19.8 6.8 %copy-start.2 = (bf16[128,512]{1,0:T(8,128)(2,1)S(1)}, bf16[128,512]{1,0:T(8,128)(2,1)}, u32[]{:S(2)}) copy-start(bf16[128,512]{1,0:T(8,128)(2,1)} %refs_2_.1) | copy-start | bytes 393220
  19.8 6.8 %copy-start.3 = (bf16[512,128]{1,0:T(8,128)(2,1)S(1)}, bf16[512,128]{1,0:T(8,128)(2,1)}, u32[]{:S(2)}) copy-start(bf16[512,128]{1,0:T(8,128)(2,1)} %refs_3_.1) | copy-start | bytes 393220
  19.8 9.5 %copy-start.1 = (bf16[256,128]{1,0:T(8,128)(2,1)S(1)}, bf16[256,128]{1,0:T(8,128)(2,1)}, u32[]{:S(2)}) copy-start(bf16[256,128]{1,0:T(8,128)(2,1)} %w_out.11) | copy-start | bytes 196612
  27.1 3.2 %collective-permute-start.7 = (bf16[2,256,128]{2,1,0:T(8,128)(2,1)S(1)}, bf16[2,256,128]{2,1,0:T(8,128)(2,1)S(1)}, u32[]{:S(2)}, u32[]{:S(2)}) collective-permute-start(bf16[2,256,128]{2,1,0:T(8,128)(2,1)S(1)} %yz_mlp.1.refs_0_), channel_id=1, source_target_pairs={{0,1},{1,0},{2,3},{3,2},{4,5},{5,4},{6,7},{7,6},{8,9},{9,8},{10,11... | collective-permute-start | bytes 393224 | tf_op jit(solution)/shard_map/ppermute | solution.py:430
  27.2 5.2 %collective-permute-start.6 = (bf16[2,256,128]{2,1,0:T(8,128)(2,1)S(1)}, bf16[2,256,128]{2,1,0:T(8,128)(2,1)S(1)}, u32[]{:S(2)}, u32[]{:S(2)}) collective-permute-start(bf16[2,256,128]{2,1,0:T(8,128)(2,1)S(1)} %yz_mlp.1.refs_0_), channel_id=1, source_target_pairs={{0,3},{1,2},{2,1},{3,0},{4,7},{5,6},{6,5},{7,4},{8,11},{9,10},{10,... | collective-permute-start | bytes 393224 | tf_op jit(solution)/shard_map/ppermute | solution.py:430
  28.9 6.6 %collective-permute-start.9 = (bf16[2,256,128]{2,1,0:T(8,128)(2,1)S(1)}, bf16[2,256,128]{2,1,0:T(8,128)(2,1)S(1)}, u32[]{:S(2)}, u32[]{:S(2)}) collective-permute-start(bf16[2,256,128]{2,1,0:T(8,128)(2,1)S(1)} %yz_mlp.1.refs_0_), channel_id=1, source_target_pairs={{0,5},{1,4},{2,7},{3,6},{4,1},{5,0},{6,3},{7,2},{8,13},{9,12},{10,... | collective-permute-start | bytes 393224 | tf_op jit(solution)/shard_map/ppermute | solution.py:430
  32.5 3.7 %collective-permute-start.8 = (bf16[2,256,128]{2,1,0:T(8,128)(2,1)S(1)}, bf16[2,256,128]{2,1,0:T(8,128)(2,1)S(1)}, u32[]{:S(2)}, u32[]{:S(2)}) collective-permute-start(bf16[2,256,128]{2,1,0:T(8,128)(2,1)S(1)} %collective-permute-done.6.refs_0_), channel_id=1, source_target_pairs={{0,1},{1,0},{2,3},{3,2},{4,5},{5,4},{6,7},{7,6},{8,9},{9,8},{10,11... | collective-permute-start | bytes 393224 | tf_op jit(solution)/shard_map/ppermute | solution.py:430
  33.2 6.5 %collective-permute-start.5 = (bf16[2,256,128]{2,1,0:T(8,128)(2,1)S(1)}, bf16[2,256,128]{2,1,0:T(8,128)(2,1)S(1)}, u32[]{:S(2)}, u32[]{:S(2)}) collective-permute-start(bf16[2,256,128]{2,1,0:T(8,128)(2,1)S(1)} %yz_mlp.1.refs_0_), channel_id=1, source_target_pairs={{0,7},{1,6},{2,5},{3,4},{4,3},{5,2},{6,1},{7,0},{8,15},{9,14},{10,... | collective-permute-start | bytes 393224 | tf_op jit(solution)/shard_map/ppermute | solution.py:430
  35.5 4.3 %collective-permute-start.11 = (bf16[2,256,128]{2,1,0:T(8,128)(2,1)S(1)}, bf16[2,256,128]{2,1,0:T(8,128)(2,1)S(1)}, u32[]{:S(2)}, u32[]{:S(2)}) collective-permute-start(bf16[2,256,128]{2,1,0:T(8,128)(2,1)S(1)} %collective-permute-done.9.refs_1_), channel_id=1, source_target_pairs={{0,1},{1,0},{2,3},{3,2},{4,5},{5,4},{6,7},{7,6},{8,9},{9,8},{10,11... | collective-permute-start | bytes 393224 | tf_op jit(solution)/shard_map/ppermute | solution.py:430
  39.7 2.1 %collective-permute-start.10 = (bf16[2,256,128]{2,1,0:T(8,128)(2,1)S(1)}, bf16[2,256,128]{2,1,0:T(8,128)(2,1)S(1)}, u32[]{:S(2)}, u32[]{:S(2)}) collective-permute-start(bf16[2,256,128]{2,1,0:T(8,128)(2,1)S(1)} %collective-permute-done.5.refs_1_), channel_id=1, source_target_pairs={{0,1},{1,0},{2,3},{3,2},{4,5},{5,4},{6,7},{7,6},{8,9},{9,8},{10,11... | collective-permute-start | bytes 393224 | tf_op jit(solution)/shard_map/ppermute | solution.py:430
where the time goes:
time: 43.8 us; the launch traced here: 43.7 us
  Pallas kernels  25.9 us (59%)
  starting transfers between devices  12.2 us (28%)
  waiting for transfers between devices  5.02 us (11%)
    ppermute x12, starting transfers between devices, swap(): return lax.ppermute(value, 'gx', [(i, i ^ offset) for i in range(n)])  12.2 us
    pallas_call x6, Pallas kernels, voxels(): pl.pallas_call(functools.partial(voxel_body, n, groups, before, last), in...  8.97 us
    pallas_call x1, Pallas kernels, first_layer(): pl.pallas_call(first_body, in_specs=[vmem] * 4, out_specs=vmem, out_shape...  5.79 us
    ppermute x12, waiting for transfers between devices, swap(): return lax.ppermute(value, 'gx', [(i, i ^ offset) for i in range(n)])  5.02 us
    pallas_call x1, Pallas kernels, partials(): pl.pallas_call(functools.partial(partial_body, n, split), in_specs=[smem,...  3.64 us
    pallas_call x1, Pallas kernels, pools(): pl.pallas_call(pool_body, in_specs=[vmem] * 2, out_specs=[vmem] * 2, out_...  3.51 us
    pallas_call x1, Pallas kernels, partials(): pl.pallas_call(functools.partial(own_body, n), in_specs=[smem] + [vmem] *...  1.74 us
    pallas_call x1, Pallas kernels, planes(): pl.pallas_call(planes_body, in_specs=[vmem] * 6, out_specs=[vmem] * 2, ou...  1.66 us
  transfers between devices with their start and end apart: 12, of which 5 were waited for; matrix products, arithmetic and copies ran while one was open for 0% of the time, Pallas kernels for 45%

commit v1 on v0

--- a/solution.py
+++ b/solution.py
@@ -380,10 +380,10 @@
 
         def chunk(j, _, yz_ref=yz_ref, pos0=pos0, slot=slot):
             home = offset(pos0 + j, n) ^ me_ref[0]
-            for x in range(0, rows, rows):
-                hidden = silu(first_ref[home, x : x + rows] + own_ref[slot + j][None]).astype(BF)
-                cells = jnp.dot(hidden.reshape(rows * ys * zs, -1), w_out[...], preferred_element_type=F32).astype(BF)
-                done_ref[slot + j, x : x + rows] = cells.reshape(rows, ys, zs, chans)
+            for x in range(0, rows, 6):
+                hidden = silu((first_ref[home, x : x + 6] + own_ref[slot + j][None]).astype(BF)).astype(BF)
+                cells = jnp.dot(hidden.reshape(6 * ys * zs, -1), w_out[...], preferred_element_type=F32).astype(BF)
+                done_ref[slot + j, x : x + 6] = cells.reshape(6, ys, zs, chans)
             if last:
                 send(done_ref, slot + j, pos0 + j, len(before) + slot + j).start()
 
@@ -467,8 +467,7 @@
     call = functools.partial(voxels, me=me, shape=features.shape, first=first, w_in=voxel_in, w_out=voxel_out)
     sibling = n // 2
     passed = swap(plane, n, 1)
-    state = call(None, n, [(0, slower)], [plane], False)
-    state = call(state, n, [(sibling, slower)], [passed], False)
+    state = call(None, n, [(0, slower), (sibling, slower)], [plane, passed], False)
     waiting = []
     for stage, digit in reversed(list(enumerate(digits))[1:-1]):
         arrived = []

time: 43.8 us -> 43.7 us (level)
    pallas_call x6 -> x5, Pallas kernels: 8.97 us -> 8.62 us  [voxels(): pl.pallas_call(functools.partial(voxel_body, n, groups, before, last), in...]
where the time goes in v1:
time: 43.7 us; the launch traced here: 43.5 us
  Pallas kernels  25.6 us (59%)
  starting transfers between devices  12.2 us (28%)
  waiting for transfers between devices  5.27 us (12%)
    ppermute x12, starting transfers between devices, swap(): return lax.ppermute(value, 'gx', [(i, i ^ offset) for i in range(n)])  12.2 us
    pallas_call x5, Pallas kernels, voxels(): pl.pallas_call(functools.partial(voxel_body, n, groups, before, last), in...  8.62 us
    pallas_call x1, Pallas kernels, first_layer(): pl.pallas_call(first_body, in_specs=[vmem] * 4, out_specs=vmem, out_shape...  5.79 us
    ppermute x12, waiting for transfers between devices, swap(): return lax.ppermute(value, 'gx', [(i, i ^ offset) for i in range(n)])  5.27 us
    pallas_call x1, Pallas kernels, partials(): pl.pallas_call(functools.partial(partial_body, n, split), in_specs=[smem,...  3.64 us
    pallas_call x1, Pallas kernels, pools(): pl.pallas_call(pool_body, in_specs=[vmem] * 2, out_specs=[vmem] * 2, out_...  3.51 us
    pallas_call x1, Pallas kernels, partials(): pl.pallas_call(functools.partial(own_body, n), in_specs=[smem] + [vmem] *...  1.74 us
    pallas_call x1, Pallas kernels, planes(): pl.pallas_call(planes_body, in_specs=[vmem] * 6, out_specs=[vmem] * 2, ou...  1.66 us
  transfers between devices with their start and end apart: 12, of which 5 were waited for; matrix products, arithmetic and copies ran while one was open for 0% of the time, Pallas kernels for 45%

profile of v1, /device:TPU:0, one launch (start us, length us, event | category | flops | bytes accessed | tf_op | source)
XLA Modules:
  0.0 43.5 jit_solution(17854443013499855555)
XLA Ops:
  0.0 3.6 %partials.1 = (bf16[4,528,128]{2,1,0:T(8,128)(2,1)S(1)}, f32[16,96,256]{2,1,0:T(8,128)S(1)}, bf16[6,256,16,128]{3,2,1,0:T(8,128)(2,1)S(1)}, bf16[16,256,96]{2,1,0:T(8,128)(2,1)S(1)}, f32[2,16,128]{2,1,0:T(8,128)S(1)}) custom-call(s32[1]{0:T(128)} %bitcast.me_ref, bf16[6,256,16,128]{3,2,1,0:T(8,128)(2,1)} %feat_hbm.1, s32[6,16,256]{2,1,0:T(8,128)} %bitcast.10, ...), custom_call_target="tpu_custom_call" | custom-call | flops 12582912 | bytes 3145728 | tf_op jit(solution)/shard_map/partials/pallas_call | solution.py:184
  3.7 0.6 %collective-permute-start = (bf16[4,528,128]{2,1,0:T(8,128)(2,1)S(1)}, bf16[4,528,128]{2,1,0:T(8,128)(2,1)S(1)}, u32[]{:S(2)}, u32[]{:S(2)}) collective-permute-start(bf16[4,528,128]{2,1,0:T(8,128)(2,1)S(1)} %get-tuple-element.45), channel_id=1, source_target_pairs={{0,1},{1,0},{2,3},{3,2},{4,5},{5,4},{6,7},{7,6},{8,9},{9,8},{10,11... | collective-permute-start | bytes 1622024 | tf_op jit(solution)/shard_map/ppermute | solution.py:430
  4.2 1.7 %own_partials.1 = bf16[4,528,128]{2,1,0:T(8,128)(2,1)S(1)} custom-call(s32[1]{0:T(128)} %bitcast.me_ref, bf16[6,256,16,128]{3,2,1,0:T(8,128)(2,1)S(1)} %get-tuple-element.42.feat_ref, bf16[16,256,96]{2,1,0:T(8,128)(2,1)S(1)} %get-tuple-element.43.by_cell_ref, f32[2,16,128]{2,1,0:T(8,128)S(1)} %get-tuple-element.44.seen_ref), custom_call_target="tpu_custom_call" | custom-call | flops 12582912 | bytes 3145728 | tf_op jit(solution)/shard_map/own_partials/pallas_call | solution.py:204
  5.9 0.0 copy-start.4
  6.0 0.0 copy-start.5
  6.0 0.0 copy-start.6
  6.0 0.0 copy-start.7
  6.0 0.0 copy-start
  6.0 0.0 collective-permute-done
  6.0 0.1 add_convert_fusion
  6.2 3.7 %collective-permute-start.3 = (bf16[1,528,128]{2,1,0:T(8,128)(2,1)S(1)}, bf16[1,528,128]{2,1,0:T(8,128)(2,1)S(1)}, u32[]{:S(2)}, u32[]{:S(2)}) collective-permute-start(bf16[1,528,128]{2,1,0:T(8,128)(2,1)S(1)} %get-tuple-element.79), channel_id=1, source_target_pairs={{0,7},{1,6},{2,5},{3,4},{4,3},{5,2},{6,1},{7,0},{8,15},{9,14},{10,... | collective-permute-start | bytes 405512 | tf_op jit(solution)/shard_map/ppermute | solution.py:430
  9.9 0.2 collective-permute-start.2
  10.1 0.2 collective-permute-start.1
  10.3 3.5 %pools.1 = (bf16[16,6,16,128]{3,2,1,0:T(8,128)(2,1)S(1)}, bf16[6,16,128]{2,1,0:T(8,128)(2,1)S(1)}) custom-call(bf16[6,256,16,128]{3,2,1,0:T(8,128)(2,1)S(1)} %get-tuple-element.42.feat_ref, f32[16,96,256]{2,1,0:T(8,128)S(1)} %get-tuple-element.48.by_z_ref), custom_call_target="tpu_custom_call" | custom-call | flops 201326592 | bytes 1048576 | tf_op jit(solution)/shard_map/pools/pallas_call | solution.py:256
  13.8 0.0 copy-done.4
  13.8 0.0 copy-done.5
  13.8 0.0 copy-done.6
  13.8 0.0 copy-done.7
  13.8 1.7 %planes.1 = (bf16[1536,128]{1,0:T(8,128)(2,1)S(1)}, bf16[96,128]{1,0:T(8,128)(2,1)S(1)}) custom-call(bf16[1536,128]{1,0:T(8,128)(2,1)S(1)} %bitcast.8, bf16[96,128]{1,0:T(8,128)(2,1)S(1)} %bitcast.9, bf16[128,512]{1,0:T(8,128)(2,1)S(1)} %copy-done.4, bf16[512,128]{1,0:T(8,128)(2,1)S(1)} %copy-done.5, bf16[128,512]{1,0:T(8,128)(2,1)S(1)} %copy-done.6, ...), custom_call_target="tpu_custom_call" | custom-call | flops 427819008 | bytes 1048576 | tf_op jit(solution)/shard_map/planes/pallas_call | solution.py:281
  15.5 0.0 collective-permute-done.3
  15.5 1.0 %collective-permute-done.2 = bf16[1,528,128]{2,1,0:T(8,128)(2,1)S(1)} collective-permute-done((bf16[1,528,128]{2,1,0:T(8,128)(2,1)S(1)}, bf16[1,528,128]{2,1,0:T(8,128)(2,1)S(1)}, u32[]{:S(2)}, u32[]{:S(2)}) %collective-permute-start.2) | collective-permute-done | bytes 135200 | tf_op jit(solution)/shard_map/ppermute | solution.py:430
  16.6 0.3 collective-permute-done.1
  16.9 0.1 add_convert_fusion.1.refs_0_
  17.0 2.8 %collective-permute-start.4 = (bf16[1,528,128]{2,1,0:T(8,128)(2,1)S(1)}, bf16[1,528,128]{2,1,0:T(8,128)(2,1)S(1)}, u32[]{:S(2)}, u32[]{:S(2)}) collective-permute-start(bf16[1,528,128]{2,1,0:T(8,128)(2,1)S(1)} %add_convert_fusion.1.refs_0_), channel_id=1, source_target_pairs={{0,8},{1,9},{2,10},{3,11},{4,12},{5,13},{6,14},{7,15},{8,0},{9,1},... | collective-permute-start | bytes 405512 | tf_op jit(solution)/shard_map/ppermute | solution.py:430
  19.7 0.0 copy-done
  19.8 5.8 %first_layer.1.first_ref = f32[16,6,256,256]{3,2,1,0:T(8,128)S(1)} custom-call(bf16[6,256,16,128]{3,2,1,0:T(8,128)(2,1)S(1)} %get-tuple-element.42.feat_ref, bf16[16,6,16,128]{3,2,1,0:T(8,128)(2,1)S(1)} %bitcast.6, bf16[6,16,128]{2,1,0:T(8,128)(2,1)S(1)} %bitcast.7, bf16[128,256]{1,0:T(8,128)(2,1)S(1)} %copy-done), custom_call_target="tpu_custom_call" | custom-call | flops 1610612736 | bytes 1048576 | tf_op jit(solution)/shard_map/first_layer/pallas_call | solution.py:346
  25.6 1.0 %collective-permute-done.4.refs_1_ = bf16[1,528,128]{2,1,0:T(8,128)(2,1)S(1)} collective-permute-done((bf16[1,528,128]{2,1,0:T(8,128)(2,1)S(1)}, bf16[1,528,128]{2,1,0:T(8,128)(2,1)S(1)}, u32[]{:S(2)}, u32[]{:S(2)}) %collective-permute-start.4) | collective-permute-done | bytes 135200 | tf_op jit(solution)/shard_map/ppermute | solution.py:430
  26.5 0.0 copy-done.2
  26.5 0.6 %yz_mlp.1.refs_0_ = bf16[2,256,128]{2,1,0:T(8,128)(2,1)S(1)} custom-call(bf16[1,528,128]{2,1,0:T(8,128)(2,1)S(1)} %add_convert_fusion.1.refs_0_, bf16[1,528,128]{2,1,0:T(8,128)(2,1)S(1)} %collective-permute-done.4.refs_1_, bf16[128,512]{1,0:T(8,128)(2,1)S(1)} %copy-done.2, bf16[512,128]{1,0:T(8,128)(2,1)S(1)} %copy-done.3), custom_call_target="tpu_custom_call" | custom-call | flops 134217728 | bytes 524288 | tf_op jit(solution)/shard_map/yz_mlp/pallas_call | solution.py:315
  27.1 0.1 collective-permute-start.7
  27.2 1.7 %collective-permute-start.6 = (bf16[2,256,128]{2,1,0:T(8,128)(2,1)S(1)}, bf16[2,256,128]{2,1,0:T(8,128)(2,1)S(1)}, u32[]{:S(2)}, u32[]{:S(2)}) collective-permute-start(bf16[2,256,128]{2,1,0:T(8,128)(2,1)S(1)} %yz_mlp.1.refs_0_), channel_id=1, source_target_pairs={{0,3},{1,2},{2,1},{3,0},{4,7},{5,6},{6,5},{7,4},{8,11},{9,10},{10,... | collective-permute-start | bytes 393224 | tf_op jit(solution)/shard_map/ppermute | solution.py:430
  28.9 0.3 collective-permute-start.9
  29.2 0.0 collective-permute-done.7.refs_1_
  29.2 1.9 %voxels.5 = (bf16[6,256,16,128]{3,2,1,0:T(8,128)(2,1)}, bf16[4,6,16,16,128]{4,3,2,1,0:T(8,128)(2,1)S(1)}) custom-call(s32[1]{0:T(128)} %bitcast.me_ref, f32[16,6,256,256]{3,2,1,0:T(8,128)S(1)} %first_layer.1.first_ref, bf16[128,256]{1,0:T(8,128)(2,1)S(1)} %copy-done, bf16[256,128]{1,0:T(8,128)(2,1)S(1)} %copy-done.1, ...), custom_call_target="tpu_custom_call" | custom-call | flops 805306368 | bytes 1048576 | tf_op jit(solution)/shard_map/voxels/pallas_call | solution.py:410
  31.1 1.3 %collective-permute-done.6.refs_0_ = bf16[2,256,128]{2,1,0:T(8,128)(2,1)S(1)} collective-permute-done((bf16[2,256,128]{2,1,0:T(8,128)(2,1)S(1)}, bf16[2,256,128]{2,1,0:T(8,128)(2,1)S(1)}, u32[]{:S(2)}, u32[]{:S(2)}) %collective-permute-start.6) | collective-permute-done | bytes 131104 | tf_op jit(solution)/shard_map/ppermute | solution.py:430
  32.5 0.7 %collective-permute-start.8 = (bf16[2,256,128]{2,1,0:T(8,128)(2,1)S(1)}, bf16[2,256,128]{2,1,0:T(8,128)(2,1)S(1)}, u32[]{:S(2)}, u32[]{:S(2)}) collective-permute-start(bf16[2,256,128]{2,1,0:T(8,128)(2,1)S(1)} %collective-permute-done.6.refs_0_), channel_id=1, source_target_pairs={{0,1},{1,0},{2,3},{3,2},{4,5},{5,4},{6,7},{7,6},{8,9},{9,8},{10,11... | collective-permute-start | bytes 393224 | tf_op jit(solution)/shard_map/ppermute | solution.py:430
  33.2 1.3 %collective-permute-start.5 = (bf16[2,256,128]{2,1,0:T(8,128)(2,1)S(1)}, bf16[2,256,128]{2,1,0:T(8,128)(2,1)S(1)}, u32[]{:S(2)}, u32[]{:S(2)}) collective-permute-start(bf16[2,256,128]{2,1,0:T(8,128)(2,1)S(1)} %yz_mlp.1.refs_0_), channel_id=1, source_target_pairs={{0,7},{1,6},{2,5},{3,4},{4,3},{5,2},{6,1},{7,0},{8,15},{9,14},{10,... | collective-permute-start | bytes 393224 | tf_op jit(solution)/shard_map/ppermute | solution.py:430
  34.5 1.2 %voxels.6 = (bf16[6,256,16,128]{3,2,1,0:T(8,128)(2,1)}, bf16[2,6,16,16,128]{4,3,2,1,0:T(8,128)(2,1)S(1)}) custom-call(s32[1]{0:T(128)} %bitcast.me_ref, f32[16,6,256,256]{3,2,1,0:T(8,128)S(1)} %first_layer.1.first_ref, bf16[128,256]{1,0:T(8,128)(2,1)S(1)} %copy-done, bf16[256,128]{1,0:T(8,128)(2,1)S(1)} %copy-done.1, ...), custom_call_target="tpu_custom_call", output_to_operand_aliasing={{0}: (6, {})} | custom-call | flops 402653184 | bytes 1048576 | tf_op jit(solution)/shard_map/voxels/pallas_call | solution.py:410
  35.6 0.0 collective-permute-done.9.refs_1_
  35.7 0.6 %collective-permute-start.11 = (bf16[2,256,128]{2,1,0:T(8,128)(2,1)S(1)}, bf16[2,256,128]{2,1,0:T(8,128)(2,1)S(1)}, u32[]{:S(2)}, u32[]{:S(2)}) collective-permute-start(bf16[2,256,128]{2,1,0:T(8,128)(2,1)S(1)} %collective-permute-done.9.refs_1_), channel_id=1, source_target_pairs={{0,1},{1,0},{2,3},{3,2},{4,5},{5,4},{6,7},{7,6},{8,9},{9,8},{10,11... | collective-permute-start | bytes 393224 | tf_op jit(solution)/shard_map/ppermute | solution.py:430
  36.2 0.0 collective-permute-done.8.refs_0_
  36.2 1.9 %voxels.7 = (bf16[6,256,16,128]{3,2,1,0:T(8,128)(2,1)}, bf16[4,6,16,16,128]{4,3,2,1,0:T(8,128)(2,1)S(1)}) custom-call(s32[1]{0:T(128)} %bitcast.me_ref, f32[16,6,256,256]{3,2,1,0:T(8,128)S(1)} %first_layer.1.first_ref, bf16[128,256]{1,0:T(8,128)(2,1)S(1)} %copy-done, bf16[256,128]{1,0:T(8,128)(2,1)S(1)} %copy-done.1, ...), custom_call_target="tpu_custom_call", output_to_operand_aliasing={{0}: (7, {})} | custom-call | flops 805306368 | bytes 1048576 | tf_op jit(solution)/shard_map/voxels/pallas_call | solution.py:410
  38.1 1.6 %collective-permute-done.5.refs_1_ = bf16[2,256,128]{2,1,0:T(8,128)(2,1)S(1)} collective-permute-done((bf16[2,256,128]{2,1,0:T(8,128)(2,1)S(1)}, bf16[2,256,128]{2,1,0:T(8,128)(2,1)S(1)}, u32[]{:S(2)}, u32[]{:S(2)}) %collective-permute-start.5) | collective-permute-done | bytes 131104 | tf_op jit(solution)/shard_map/ppermute | solution.py:430
  39.7 0.1 collective-permute-start.10
  39.8 0.0 collective-permute-done.11.refs_0_
  39.8 1.9 %voxels.8 = (bf16[6,256,16,128]{3,2,1,0:T(8,128)(2,1)}, bf16[4,6,16,16,128]{4,3,2,1,0:T(8,128)(2,1)S(1)}) custom-call(s32[1]{0:T(128)} %bitcast.me_ref, f32[16,6,256,256]{3,2,1,0:T(8,128)S(1)} %first_layer.1.first_ref, bf16[128,256]{1,0:T(8,128)(2,1)S(1)} %copy-done, bf16[256,128]{1,0:T(8,128)(2,1)S(1)} %copy-done.1, ...), custom_call_target="tpu_custom_call", output_to_operand_aliasing={{0}: (7, {})} | custom-call | flops 805306368 | bytes 1048576 | tf_op jit(solution)/shard_map/voxels/pallas_call | solution.py:410
  41.7 0.0 collective-permute-done.10.refs_0_
  41.7 1.8 %voxels.9 = bf16[6,256,16,128]{3,2,1,0:T(8,128)(2,1)} custom-call(s32[1]{0:T(128)} %bitcast.me_ref, f32[16,6,256,256]{3,2,1,0:T(8,128)S(1)} %first_layer.1.first_ref, bf16[128,256]{1,0:T(8,128)(2,1)S(1)} %copy-done, bf16[256,128]{1,0:T(8,128)(2,1)S(1)} %copy-done.1, ...), custom_call_target="tpu_custom_call", output_to_operand_aliasing={{}: (6, {})} | custom-call | flops 402653184 | bytes 1048576 | tf_op jit(solution)/shard_map/voxels/pallas_call | solution.py:410
  (6 shorter events, 0.0 us)
Async XLA Ops:
  3.7 2.4 %collective-permute-start = (bf16[4,528,128]{2,1,0:T(8,128)(2,1)S(1)}, bf16[4,528,128]{2,1,0:T(8,128)(2,1)S(1)}, u32[]{:S(2)}, u32[]{:S(2)}) collective-permute-start(bf16[4,528,128]{2,1,0:T(8,128)(2,1)S(1)} %get-tuple-element.45), channel_id=1, source_target_pairs={{0,1},{1,0},{2,3},{3,2},{4,5},{5,4},{6,7},{7,6},{8,9},{9,8},{10,11... | collective-permute-start | bytes 1622024 | tf_op jit(solution)/shard_map/ppermute | solution.py:430
  5.9 7.9 %copy-start.4 = (bf16[128,512]{1,0:T(8,128)(2,1)S(1)}, bf16[128,512]{1,0:T(8,128)(2,1)}, u32[]{:S(2)}) copy-start(bf16[128,512]{1,0:T(8,128)(2,1)} %xy_in.1) | copy-start | bytes 393220
  6.0 7.9 %copy-start.5 = (bf16[512,128]{1,0:T(8,128)(2,1)S(1)}, bf16[512,128]{1,0:T(8,128)(2,1)}, u32[]{:S(2)}) copy-start(bf16[512,128]{1,0:T(8,128)(2,1)} %xy_out.1) | copy-start | bytes 393220
  6.0 7.9 %copy-start.6 = (bf16[128,512]{1,0:T(8,128)(2,1)S(1)}, bf16[128,512]{1,0:T(8,128)(2,1)}, u32[]{:S(2)}) copy-start(bf16[128,512]{1,0:T(8,128)(2,1)} %xz_in.1) | copy-start | bytes 393220
  6.0 7.9 %copy-start.7 = (bf16[512,128]{1,0:T(8,128)(2,1)S(1)}, bf16[512,128]{1,0:T(8,128)(2,1)}, u32[]{:S(2)}) copy-start(bf16[512,128]{1,0:T(8,128)(2,1)} %xz_out.1) | copy-start | bytes 393220
  6.0 13.8 %copy-start = (bf16[128,256]{1,0:T(8,128)(2,1)S(1)}, bf16[128,256]{1,0:T(8,128)(2,1)}, u32[]{:S(2)}) copy-start(bf16[128,256]{1,0:T(8,128)(2,1)} %w_in.11) | copy-start | bytes 196612
  6.2 9.3 %collective-permute-start.3 = (bf16[1,528,128]{2,1,0:T(8,128)(2,1)S(1)}, bf16[1,528,128]{2,1,0:T(8,128)(2,1)S(1)}, u32[]{:S(2)}, u32[]{:S(2)}) collective-permute-start(bf16[1,528,128]{2,1,0:T(8,128)(2,1)S(1)} %get-tuple-element.79), channel_id=1, source_target_pairs={{0,7},{1,6},{2,5},{3,4},{4,3},{5,2},{6,1},{7,0},{8,15},{9,14},{10,... | collective-permute-start | bytes 405512 | tf_op jit(solution)/shard_map/ppermute | solution.py:430
  9.9 6.7 %collective-permute-start.2 = (bf16[1,528,128]{2,1,0:T(8,128)(2,1)S(1)}, bf16[1,528,128]{2,1,0:T(8,128)(2,1)S(1)}, u32[]{:S(2)}, u32[]{:S(2)}) collective-permute-start(bf16[1,528,128]{2,1,0:T(8,128)(2,1)S(1)} %get-tuple-element.80), channel_id=1, source_target_pairs={{0,5},{1,4},{2,7},{3,6},{4,1},{5,0},{6,3},{7,2},{8,13},{9,12},{10,... | collective-permute-start | bytes 405512 | tf_op jit(solution)/shard_map/ppermute | solution.py:430
  10.1 6.8 %collective-permute-start.1 = (bf16[1,528,128]{2,1,0:T(8,128)(2,1)S(1)}, bf16[1,528,128]{2,1,0:T(8,128)(2,1)S(1)}, u32[]{:S(2)}, u32[]{:S(2)}) collective-permute-start(bf16[1,528,128]{2,1,0:T(8,128)(2,1)S(1)} %get-tuple-element.81), channel_id=1, source_target_pairs={{0,3},{1,2},{2,1},{3,0},{4,7},{5,6},{6,5},{7,4},{8,11},{9,10},{10,... | collective-permute-start | bytes 405512 | tf_op jit(solution)/shard_map/ppermute | solution.py:430
  17.0 9.5 %collective-permute-start.4 = (bf16[1,528,128]{2,1,0:T(8,128)(2,1)S(1)}, bf16[1,528,128]{2,1,0:T(8,128)(2,1)S(1)}, u32[]{:S(2)}, u32[]{:S(2)}) collective-permute-start(bf16[1,528,128]{2,1,0:T(8,128)(2,1)S(1)} %add_convert_fusion.1.refs_0_), channel_id=1, source_target_pairs={{0,8},{1,9},{2,10},{3,11},{4,12},{5,13},{6,14},{7,15},{8,0},{9,1},... | collective-permute-start | bytes 405512 | tf_op jit(solution)/shard_map/ppermute | solution.py:430
  19.8 6.8 %copy-start.2 = (bf16[128,512]{1,0:T(8,128)(2,1)S(1)}, bf16[128,512]{1,0:T(8,128)(2,1)}, u32[]{:S(2)}) copy-start(bf16[128,512]{1,0:T(8,128)(2,1)} %refs_2_.1) | copy-start | bytes 393220
  19.8 6.8 %copy-start.3 = (bf16[512,128]{1,0:T(8,128)(2,1)S(1)}, bf16[512,128]{1,0:T(8,128)(2,1)}, u32[]{:S(2)}) copy-start(bf16[512,128]{1,0:T(8,128)(2,1)} %refs_3_.1) | copy-start | bytes 393220
  19.8 9.5 %copy-start.1 = (bf16[256,128]{1,0:T(8,128)(2,1)S(1)}, bf16[256,128]{1,0:T(8,128)(2,1)}, u32[]{:S(2)}) copy-start(bf16[256,128]{1,0:T(8,128)(2,1)} %w_out.9) | copy-start | bytes 196612
  27.1 2.1 %collective-permute-start.7 = (bf16[2,256,128]{2,1,0:T(8,128)(2,1)S(1)}, bf16[2,256,128]{2,1,0:T(8,128)(2,1)S(1)}, u32[]{:S(2)}, u32[]{:S(2)}) collective-permute-start(bf16[2,256,128]{2,1,0:T(8,128)(2,1)S(1)} %yz_mlp.1.refs_0_), channel_id=1, source_target_pairs={{0,1},{1,0},{2,3},{3,2},{4,5},{5,4},{6,7},{7,6},{8,9},{9,8},{10,11... | collective-permute-start | bytes 393224 | tf_op jit(solution)/shard_map/ppermute | solution.py:430
  27.2 5.2 %collective-permute-start.6 = (bf16[2,256,128]{2,1,0:T(8,128)(2,1)S(1)}, bf16[2,256,128]{2,1,0:T(8,128)(2,1)S(1)}, u32[]{:S(2)}, u32[]{:S(2)}) collective-permute-start(bf16[2,256,128]{2,1,0:T(8,128)(2,1)S(1)} %yz_mlp.1.refs_0_), channel_id=1, source_target_pairs={{0,3},{1,2},{2,1},{3,0},{4,7},{5,6},{6,5},{7,4},{8,11},{9,10},{10,... | collective-permute-start | bytes 393224 | tf_op jit(solution)/shard_map/ppermute | solution.py:430
  28.9 6.8 %collective-permute-start.9 = (bf16[2,256,128]{2,1,0:T(8,128)(2,1)S(1)}, bf16[2,256,128]{2,1,0:T(8,128)(2,1)S(1)}, u32[]{:S(2)}, u32[]{:S(2)}) collective-permute-start(bf16[2,256,128]{2,1,0:T(8,128)(2,1)S(1)} %yz_mlp.1.refs_0_), channel_id=1, source_target_pairs={{0,5},{1,4},{2,7},{3,6},{4,1},{5,0},{6,3},{7,2},{8,13},{9,12},{10,... | collective-permute-start | bytes 393224 | tf_op jit(solution)/shard_map/ppermute | solution.py:430
  32.5 3.8 %collective-permute-start.8 = (bf16[2,256,128]{2,1,0:T(8,128)(2,1)S(1)}, bf16[2,256,128]{2,1,0:T(8,128)(2,1)S(1)}, u32[]{:S(2)}, u32[]{:S(2)}) collective-permute-start(bf16[2,256,128]{2,1,0:T(8,128)(2,1)S(1)} %collective-permute-done.6.refs_0_), channel_id=1, source_target_pairs={{0,1},{1,0},{2,3},{3,2},{4,5},{5,4},{6,7},{7,6},{8,9},{9,8},{10,11... | collective-permute-start | bytes 393224 | tf_op jit(solution)/shard_map/ppermute | solution.py:430
  33.2 6.5 %collective-permute-start.5 = (bf16[2,256,128]{2,1,0:T(8,128)(2,1)S(1)}, bf16[2,256,128]{2,1,0:T(8,128)(2,1)S(1)}, u32[]{:S(2)}, u32[]{:S(2)}) collective-permute-start(bf16[2,256,128]{2,1,0:T(8,128)(2,1)S(1)} %yz_mlp.1.refs_0_), channel_id=1, source_target_pairs={{0,7},{1,6},{2,5},{3,4},{4,3},{5,2},{6,1},{7,0},{8,15},{9,14},{10,... | collective-permute-start | bytes 393224 | tf_op jit(solution)/shard_map/ppermute | solution.py:430
  35.7 4.2 %collective-permute-start.11 = (bf16[2,256,128]{2,1,0:T(8,128)(2,1)S(1)}, bf16[2,256,128]{2,1,0:T(8,128)(2,1)S(1)}, u32[]{:S(2)}, u32[]{:S(2)}) collective-permute-start(bf16[2,256,128]{2,1,0:T(8,128)(2,1)S(1)} %collective-permute-done.9.refs_1_), channel_id=1, source_target_pairs={{0,1},{1,0},{2,3},{3,2},{4,5},{5,4},{6,7},{7,6},{8,9},{9,8},{10,11... | collective-permute-start | bytes 393224 | tf_op jit(solution)/shard_map/ppermute | solution.py:430
  39.7 2.0 %collective-permute-start.10 = (bf16[2,256,128]{2,1,0:T(8,128)(2,1)S(1)}, bf16[2,256,128]{2,1,0:T(8,128)(2,1)S(1)}, u32[]{:S(2)}, u32[]{:S(2)}) collective-permute-start(bf16[2,256,128]{2,1,0:T(8,128)(2,1)S(1)} %collective-permute-done.5.refs_1_), channel_id=1, source_target_pairs={{0,1},{1,0},{2,3},{3,2},{4,5},{5,4},{6,7},{7,6},{8,9},{9,8},{10,11... | collective-permute-start | bytes 393224 | tf_op jit(solution)/shard_map/ppermute | solution.py:430
